TPU v7x, 512 devices: a whole 4x8x8 slice. The times are simulated.
512 devices in a mesh: tile: 128 (over y, x, z_hi), src: 4 (over z_lo, core).
Axes of the slice: x: 4, y: 8, z: 8 (z_hi: 4, z_lo: 2; z = z_hi * 2 + z_lo), core: 2. Of those that a mesh axis runs over, the one named last changes fastest.
Arguments:
- mask_tiles: int32 [2048, 512], P('tile'), may hold values 0 or 1
- kernels: bfloat16 [16, 3, 8, 2, 17, 17], P('src'), may hold values from -0.5 to 0.5
- source_weight: int32 [16], P('src'), may hold values from 1 to 8
- dill_rate: float32 [8], P('src'), may hold values from 0.3 to 3
- quencher_load: float32 [8], P('src'), may hold values from 0.1 to 0.5
Outputs:
- acid_field: float32 [8, 2048, 512], P('src', 'tile')
- inhibitor: float32 [8, 2048, 512], P('src', 'tile')
All inputs are finite; a program needn't handle non-finite values. No bound on the sum of `mask_tiles` on one device may be relied on, other than what follows from the above.
Results may differ from a plain program's by a relative error of at most 0.0008.
Values may be sent and summed in bfloat16 or wider, within the bound.
No kernel may reach another device: no remote copies, remote signals or barrier semaphores. Data moves between devices by JAX's collectives and lax.ppermute only.
A program may use at most 64 MiB of HBM per device.

v0:
```python
import jax
import jax.numpy as jnp
from jax import lax
from jax.experimental import pallas as pl
from jax.experimental.pallas import tpu as pltpu
from jax.sharding import PartitionSpec as P

STEPS = 8
KS = 17
TAPS = KS * KS
KPAD = 304
WCOL = 304
WLANES = 384
COLS = 512
TILES = COLS // 128
OWN = 16
ROWS = OWN + 2 * STEPS
BAND = ROWS + KS - 1
PLANES = 8

acid_lateral = 0.15
acid_vertical = 0.12
quench_lateral = 0.05
quench_vertical = 0.04
react_rate = 0.3
deprotect_rate = 0.25


def image_kernel(up_ref, mask_ref, down_ref, w_ref, out_ref, x_ref, b_ref, i_ref):
    f32 = jnp.float32
    x_ref[...] = jnp.zeros_like(x_ref)
    x_ref[0:16, 128:640] = up_ref[...].astype(f32)
    x_ref[16:32, 128:640] = mask_ref[...].astype(f32)
    x_ref[32:48, 128:640] = down_ref[...].astype(f32)
    filled = BAND * KS
    b_ref[:, filled:, :] = jnp.zeros((TILES, b_ref.shape[1] - filled, 128), f32)
    for b in range(KS):
        for t in range(TILES):
            start = 120 + b + 128 * t
            b_ref[t, pl.ds(b, BAND, stride=KS), :] = x_ref[:, start : start + 128]
    w_all = w_ref[...].reshape(192, WLANES)
    weight = w_all[:, WCOL : WCOL + 1].astype(f32)
    w_taps = w_all[:, :KPAD]

    def body(q, carry):
        base = pl.multiple_of(q * (8 * KS), 8)
        view = b_ref.at[:, pl.ds(base, 440), :]
        for d in range(8):
            patches = jnp.concatenate(
                [view[t, KS * d : KS * d + KPAD, :] for t in range(TILES)], axis=1
            ).astype(jnp.bfloat16)
            field = jnp.dot(w_taps, patches, preferred_element_type=f32)
            power = (field * field * weight).reshape(4, 2, 3, 8, COLS)
            total = power.sum(axis=(0, 2)).sum(axis=1)
            for k in range(2):
                i_ref[k, pl.ds(q * 8 + d, 1), :] = total[k : k + 1]
        return carry

    lax.fori_loop(0, ROWS // 8, body, 0)
    out_ref[...] = i_ref[...].astype(jnp.bfloat16)


def bake_kernel(scale, g_ref, w_ref, acid_ref, inhib_ref, a_ref, q_ref, d_ref):
    f32 = jnp.float32
    tile = lax.axis_index("tile")
    src = lax.axis_index("src")
    has_up = jnp.where(tile > 0, 1.0, 0.0).astype(f32)
    has_down = jnp.where(tile < lax.axis_size("tile") - 1, 1.0, 0.0).astype(f32)
    par = w_ref[0, 0:16, :].astype(f32)
    for s in range(1, 4):
        par = par + w_ref[s, 0:16, :].astype(f32)
    par = par[0:8]

    def column(first):
        return par[:, first : first + 1] + par[:, first + 1 : first + 2] + par[:, first + 2 : first + 3]

    dill = jnp.broadcast_to(column(WCOL + 1) * scale, (8, 128))
    quench = jnp.broadcast_to(column(WCOL + 4), (8, 128))
    for k in range(PLANES):
        plane = g_ref[k // 2, k % 2].astype(f32)
        for t in range(TILES):
            a_ref[0, t, pl.ds(k, ROWS, stride=PLANES), :] = plane[:, 128 * t : 128 * t + 128]
    for r in range(ROWS):
        for t in range(TILES):
            cut = slice(8 * r, 8 * r + 8)
            acid = 1.0 - jnp.exp(-dill * a_ref[0, t, cut, :])
            load = quench
            if r < STEPS:
                acid, load = acid * has_up, load * has_up
            elif r >= STEPS + OWN:
                acid, load = acid * has_down, load * has_down
            a_ref[0, t, cut, :] = acid
            q_ref[0, t, cut, :] = load

    lane = lax.broadcasted_iota(jnp.int32, (8, 128), 1)
    sub = lax.broadcasted_iota(jnp.int32, (8, 128), 0)
    first_lane, last_lane = lane == 0, lane == 127
    first_sub, last_sub = sub == 0, sub == 7
    zero = jnp.zeros((8, 128), f32)

    def spread(ref, now, r):
        def rows(at):
            start = pl.multiple_of(at * 8, 8)
            return [ref[now, t, pl.ds(start, 8), :] for t in range(TILES)]

        above, here, below = rows(r - 1), rows(r), rows(r + 1)
        right = [pltpu.roll(v, 1, 1) for v in here]
        left = [pltpu.roll(v, 127, 1) for v in here]
        lateral, vertical = [], []
        for t in range(TILES):
            before = right[t - 1] if t > 0 else zero
            after = left[t + 1] if t < TILES - 1 else zero
            side = jnp.where(first_lane, before, right[t]) + jnp.where(last_lane, after, left[t])
            lateral.append(side + (above[t] + below[t]))
            lower = jnp.where(first_sub, here[t], pltpu.roll(here[t], 1, 0))
            upper = jnp.where(last_sub, here[t], pltpu.roll(here[t], 7, 0))
            vertical.append(lower + upper)
        return here, lateral, vertical

    acid_keep = 1.0 - 4.0 * acid_lateral - 2.0 * acid_vertical
    quench_keep = 1.0 - 4.0 * quench_lateral - 2.0 * quench_vertical
    for step in range(STEPS):
        now, later = step % 2, (step + 1) % 2
        first, last = step + 1, ROWS - 1 - step

        def body(r, carry):
            acid, acid_side, acid_up = spread(a_ref, now, r)
            load, load_side, load_up = spread(q_ref, now, r)
            keep = jnp.where(r < STEPS, has_up, jnp.where(r >= STEPS + OWN, has_down, 1.0))
            start = pl.multiple_of(r * 8, 8)
            for t in range(TILES):
                reacted = (react_rate * acid[t]) * load[t]
                new_acid = acid_keep * acid[t] + acid_lateral * acid_side[t] + acid_vertical * acid_up[t] - reacted
                new_load = quench_keep * load[t] + quench_lateral * load_side[t] + quench_vertical * load_up[t] - reacted
                new_acid = new_acid * keep
                a_ref[later, t, pl.ds(start, 8), :] = new_acid
                q_ref[later, t, pl.ds(start, 8), :] = new_load * keep
                if step == 0:
                    d_ref[t, pl.ds(start, 8), :] = new_acid
                else:
                    d_ref[t, pl.ds(start, 8), :] = d_ref[t, pl.ds(start, 8), :] + new_acid
            return carry

        lax.fori_loop(first, last, body, 0, unroll=2)

    end = STEPS % 2
    for s in range(4):

        @pl.when(src == s)
        def _():
            for k in range(2):
                rows = pl.ds(8 * STEPS + 2 * s + k, OWN, stride=PLANES)
                for t in range(TILES):
                    cut = slice(128 * t, 128 * t + 128)
                    acid_ref[k, :, cut] = a_ref[end, t, rows, :]
                    inhib_ref[k, :, cut] = jnp.exp(-deprotect_rate * d_ref[t, rows, :])


def pieces(x):
    out, rest = [], x
    for _ in range(3):
        part = lax.reduce_precision(rest, 8, 7)
        out.append(part.astype(jnp.bfloat16))
        rest = rest - part
    return out


def shards(mask_tiles, kernels, source_weight, dill_rate, quencher_load):
    bf16 = jnp.bfloat16
    tiles = lax.axis_size("tile")
    sources = kernels.shape[0]
    up = lax.ppermute(mask_tiles, "tile", [(i, i + 1) for i in range(tiles - 1)])
    down = lax.ppermute(mask_tiles, "tile", [(i + 1, i) for i in range(tiles - 1)])

    taps = kernels.reshape(sources, 3, 4, 2, 2, KS, KS).transpose(2, 3, 0, 1, 4, 5, 6).reshape(4, 48, TAPS)
    weight = jnp.broadcast_to(source_weight.astype(bf16)[None, None, :, None], (4, 2, sources, 6)).reshape(4, 48, 1)
    position = lax.axis_index("src") * 2
    values = jnp.stack(pieces(dill_rate) + pieces(quencher_load), axis=1)
    values = lax.dynamic_update_slice(jnp.zeros((48, 6), bf16), values, (position, 0))
    values = jnp.broadcast_to(values[None], (4, 48, 6))
    rest = WLANES - WCOL - 7
    packed = jnp.concatenate(
        [taps, jnp.zeros((4, 48, WCOL - TAPS), bf16), weight, values, jnp.zeros((4, 48, rest), bf16)], axis=2
    )
    w_own = lax.all_to_all(packed, "src", 0, 0)

    intensity = pl.pallas_call(
        image_kernel,
        out_shape=jax.ShapeDtypeStruct((2, ROWS, COLS), bf16),
        scratch_shapes=[
            pltpu.VMEM((BAND, COLS + 256), jnp.float32),
            pltpu.VMEM((TILES, 848, 128), jnp.float32),
            pltpu.VMEM((2, ROWS, COLS), jnp.float32),
        ],
        compiler_params=pltpu.CompilerParams(vmem_limit_bytes=32 * 1024 * 1024),
        name="image",
    )(up, mask_tiles, down, w_own)
    gathered = lax.all_gather(intensity, "src")
    scale = 1.0 / (24.0 * sources * lax.axis_size("src"))

    def bake(*refs):
        bake_kernel(scale, *refs)

    out = jax.ShapeDtypeStruct((2, OWN, COLS), jnp.float32)
    acid, inhibitor = pl.pallas_call(
        bake,
        out_shape=(out, out),
        scratch_shapes=[
            pltpu.VMEM((2, TILES, ROWS * PLANES, 128), jnp.float32),
            pltpu.VMEM((2, TILES, ROWS * PLANES, 128), jnp.float32),
            pltpu.VMEM((TILES, ROWS * PLANES, 128), jnp.float32),
        ],
        compiler_params=pltpu.CompilerParams(vmem_limit_bytes=32 * 1024 * 1024),
        name="bake",
    )(gathered, w_own)
    return acid, inhibitor


def solution(mesh):
    in_specs = (
        P("tile", None),
        P("src", None, None, None, None, None),
        P("src"),
        P("src"),
        P("src"),
    )
    out_specs = (P("src", "tile", None), P("src", "tile", None))
    return jax.shard_map(shards, mesh=mesh, in_specs=in_specs, out_specs=out_specs, check_vma=False)
```

profile of v0, /device:TPU:49, one launch (start us, length us, event | category | flops | bytes accessed | tf_op | source)
XLA Modules:
  0.0 49.2 jit_solution(15414818945225952063)
XLA Ops:
  0.6 0.7 %fusion.4 = (bf16[2,1]{0,1:T(2,128)(2,1)S(1)}, bf16[2,1]{0,1:T(2,128)(2,1)S(1)}, bf16[2,1]{0,1:T(2,128)(2,1)S(1)}) fusion(f32[2]{0:T(128)} %param.8), kind=kLoop, calls=%fused_computation.13 | loop fusion | flops 16 | bytes 20 | tf_op jit(solution)/shard_map/stack | solution.py:178
  1.3 0.1 copy.12
  1.4 0.1 copy.13
  1.5 0.1 copy.14
  1.6 0.7 %fusion.9 = (bf16[2,1]{0,1:T(2,128)(2,1)S(1)}, bf16[2,1]{0,1:T(2,128)(2,1)S(1)}, bf16[2,1]{0,1:T(2,128)(2,1)S(1)}) fusion(f32[2]{0:T(128)} %param.9), kind=kLoop, calls=%fused_computation.18 | loop fusion | flops 16 | bytes 20 | tf_op jit(solution)/shard_map/stack | solution.py:178
  2.3 0.1 copy.15
  2.4 0.1 copy.16
  2.5 0.1 copy.17
  2.6 0.0 copy-start.1
  2.6 1.4 %copy.19 = bf16[4,3,4,2,2,17,17]{6,5,4,1,0,3,2:T(8,128)(2,1)S(1)} copy(bf16[4,3,4,2,2,17,17]{6,4,5,3,2,1,0:T(2,128)(2,1)} %bitcast.19) | data formatting | bytes 221952 | tf_op jit(solution)/shard_map/reshape | solution.py:175
  4.0 0.0 copy-start
  4.0 0.6 %reshape.19 = bf16[4,48,289]{2,1,0:T(8,128)(2,1)S(1)} reshape(bf16[4,2,4,3,2,17,17]{6,5,4,3,2,1,0:T(8,128)(2,1)S(1)} %bitcast.18) | data formatting | bytes 221952 | tf_op jit(solution)/shard_map/reshape | solution.py:175
  4.6 0.0 copy-done.1
  4.6 0.1 broadcast_in_dim.26
  4.7 0.1 broadcast_in_dim.27
  4.8 0.1 stack.27
  4.9 0.1 broadcast_in_dim.28
  5.0 0.8 %concatenate.3 = bf16[4,48,384]{2,1,0:T(8,128)(2,1)} concatenate(bf16[4,48,289]{2,1,0:T(8,128)(2,1)S(1)} %reshape.19, bf16[4,48,15]{2,1,0:T(8,128)(2,1)S(1)} %broadcast_in_dim.25, bf16[4,48,1]{2,1,0:T(8,128)(2,1)S(1)} %broadcast_in_dim.28, bf16[4,48,6]{2,1,0:T(8,128)(2,1)S(1)} %broadcast_in_dim.30, bf16[4,48,73]{2,1,0:T(8,128)(2,1)S(1)} %broadcast_in_dim.31), dimensions={2} | concatenate | bytes 294912 | tf_op jit(solution)/shard_map/concatenate | solution.py:182
  5.8 4.3 %all-to-all-start = ((bf16[4,48,384]{2,1,0:T(8,128)(2,1)}), bf16[4,48,384]{2,1,0:T(8,128)(2,1)S(1)}, u32[]{:S(2)}, u32[]{:S(2)}) async-start(bf16[4,48,384]{2,1,0:T(8,128)(2,1)} %concatenate.3), calls=%async_computation | async-start | bytes 294912 | tf_op jit(solution)/shard_map/all_to_all | solution.py:185
  10.1 0.0 copy-done
  10.1 5.8 %collective-permute-start = (s32[16,512]{1,0:T(8,128)S(1)}, s32[16,512]{1,0:T(8,128)S(1)}, u32[]{:S(2)}, u32[]{:S(2)}) collective-permute-start(s32[16,512]{1,0:T(8,128)S(1)} %copy-done), channel_id=1, source_target_pairs={{0,4},{4,8},{8,12},{12,16},{16,20},{20,24},{24,28},{28,32},{32,36}... | collective-permute-start | bytes 98312 | tf_op jit(solution)/shard_map/ppermute | solution.py:172
  15.9 9.4 %collective-permute-start.1 = (s32[16,512]{1,0:T(8,128)S(1)}, s32[16,512]{1,0:T(8,128)S(1)}, u32[]{:S(2)}, u32[]{:S(2)}) collective-permute-start(s32[16,512]{1,0:T(8,128)S(1)} %copy-done), channel_id=1, source_target_pairs={{4,0},{8,4},{12,8},{16,12},{20,16},{24,20},{28,24},{32,28},{36,32}... | collective-permute-start | bytes 98312 | tf_op jit(solution)/shard_map/ppermute | solution.py:173
  25.3 0.0 collective-permute-done.up_ref
  25.4 1.0 %collective-permute-done.1.down_ref = s32[16,512]{1,0:T(8,128)S(1)} collective-permute-done((s32[16,512]{1,0:T(8,128)S(1)}, s32[16,512]{1,0:T(8,128)S(1)}, u32[]{:S(2)}, u32[]{:S(2)}) %collective-permute-start.1) | collective-permute-done | bytes 32800 | tf_op jit(solution)/shard_map/ppermute | solution.py:173
  26.3 0.0 all-to-all-done.w_ref.refs_1_
  26.3 4.9 %image.1 = bf16[2,32,512]{2,1,0:T(8,128)(2,1)S(1)} custom-call(s32[16,512]{1,0:T(8,128)S(1)} %collective-permute-done.up_ref, s32[16,512]{1,0:T(8,128)S(1)} %copy-done, s32[16,512]{1,0:T(8,128)S(1)} %collective-permute-done.1.down_ref, bf16[4,48,384]{2,1,0:T(8,128)(2,1)S(1)} %all-to-all-done.w_ref.refs_1_), custom_call_target="tpu_custom_call" | custom-call | tf_op jit(solution)/shard_map/image/pallas_call | solution.py:187
  31.3 7.0 %all-gather = bf16[8,32,512]{2,1,0:T(8,128)(2,1)S(1)} all-gather(bf16[2,32,512]{2,1,0:T(8,128)(2,1)S(1)} %image.1), channel_id=2, replica_groups=mesh['tile'=128,'src'=4] {'src'}, dimensions={0}, use_global_device_ids=true | all-gather | bytes 327680 | tf_op jit(solution)/shard_map/all_gather | solution.py:198
  38.3 10.9 %bake.1 = (f32[2,16,512]{2,1,0:T(8,128)}, f32[2,16,512]{2,1,0:T(8,128)}) custom-call(bf16[4,2,32,512]{3,2,1,0:T(8,128)(2,1)S(1)} %bitcast.17, bf16[4,48,384]{2,1,0:T(8,128)(2,1)S(1)} %all-to-all-done.w_ref.refs_1_), custom_call_target="tpu_custom_call" | custom-call | tf_op jit(solution)/shard_map/bake/pallas_call | solution.py:205
  (6 shorter events, 0.0 us)
Async XLA Ops:
  2.6 2.0 %copy-start.1 = (s32[4]{0:T(128)S(1)}, s32[4]{0:T(128)}, u32[]{:S(2)}) copy-start(s32[4]{0:T(128)} %param.7) | copy-start | bytes 52
  4.0 6.1 %copy-start = (s32[16,512]{1,0:T(8,128)S(1)}, s32[16,512]{1,0:T(8,128)}, u32[]{:S(2)}) copy-start(s32[16,512]{1,0:T(8,128)} %mask_ref.1) | copy-start | bytes 98308
  5.8 20.5 %all-to-all-start = ((bf16[4,48,384]{2,1,0:T(8,128)(2,1)}), bf16[4,48,384]{2,1,0:T(8,128)(2,1)S(1)}, u32[]{:S(2)}, u32[]{:S(2)}) async-start(bf16[4,48,384]{2,1,0:T(8,128)(2,1)} %concatenate.3), calls=%async_computation | async-start | bytes 294912 | tf_op jit(solution)/shard_map/all_to_all | solution.py:185
  10.1 15.2 %collective-permute-start = (s32[16,512]{1,0:T(8,128)S(1)}, s32[16,512]{1,0:T(8,128)S(1)}, u32[]{:S(2)}, u32[]{:S(2)}) collective-permute-start(s32[16,512]{1,0:T(8,128)S(1)} %copy-done), channel_id=1, source_target_pairs={{0,4},{4,8},{8,12},{12,16},{16,20},{20,24},{24,28},{28,32},{32,36}... | collective-permute-start | bytes 98312 | tf_op jit(solution)/shard_map/ppermute | solution.py:172
  15.9 10.4 %collective-permute-start.1 = (s32[16,512]{1,0:T(8,128)S(1)}, s32[16,512]{1,0:T(8,128)S(1)}, u32[]{:S(2)}, u32[]{:S(2)}) collective-permute-start(s32[16,512]{1,0:T(8,128)S(1)} %copy-done), channel_id=1, source_target_pairs={{4,0},{8,4},{12,8},{16,12},{20,16},{24,20},{28,24},{32,28},{36,32}... | collective-permute-start | bytes 98312 | tf_op jit(solution)/shard_map/ppermute | solution.py:173
where the time goes:
time: 49.5 us; the launch traced here: 49.2 us
  starting transfers between devices  19.5 us (39%)
  Pallas kernels  15.9 us (32%)
  blocking collectives  6.97 us (14%)
  local copies, waits for them, and re-layouts  3.77 us (8%)
  other arithmetic  1.33 us (3%)
  waiting for transfers between devices  1 us (2%)
  between operations  0.74 us (1%)
    pallas_call x1, Pallas kernels, shards(): pl.pallas_call(bake, out_shape=(out, out), scratch_shapes=[pltpu.VMEM((2,...  10.9 us
    ppermute x1, starting transfers between devices, shards(): lax.ppermute(mask_tiles, 'tile', [(i + 1, i) for i in range(tiles - 1)])  9.41 us
    all_gather x1, blocking collectives, shards(): gathered = lax.all_gather(intensity, 'src')  6.97 us
    ppermute x1, starting transfers between devices, shards(): lax.ppermute(mask_tiles, 'tile', [(i, i + 1) for i in range(tiles - 1)])  5.8 us
    pallas_call x1, Pallas kernels, shards(): pl.pallas_call(image_kernel, out_shape=jax.ShapeDtypeStruct((2, ROWS, COL...  4.93 us
    all_to_all x1, starting transfers between devices, shards(): w_own = lax.all_to_all(packed, 'src', 0, 0)  4.31 us
    reshape x2, local copies, waits for them, and re-layouts, shards(): kernels.reshape(sources, 3, 4, 2, 2, KS, KS).transpose(2, 3, 0, 1, 4, 5, 6)  1.95 us
    another operation x2, other arithmetic, shards(): values = jnp.stack(pieces(dill_rate) + pieces(quencher_load), axis=1)  1.32 us
  transfers between devices with their start and end apart: 3, of which 1 were waited for; matrix products, arithmetic and copies ran while one was open for 0% of the time, Pallas kernels for 0%

commit v1 on v0

v1 whole, which is shorter than its diff:
```python
import jax
import jax.numpy as jnp
from jax import lax
from jax.experimental import pallas as pl
from jax.experimental.pallas import tpu as pltpu
from jax.sharding import PartitionSpec as P

STEPS = 8
KS = 17
TAPS = KS * KS
KPAD = 304
WCOL = 304
WLANES = 384
COLS = 512
TILES = COLS // 128
OWN = 16
HALF = 16
ROWS = OWN + 2 * STEPS
PLANES = 8
GROUPS = 4
PARAMS = 64

acid_lateral = 0.15
acid_vertical = 0.12
quench_lateral = 0.05
quench_vertical = 0.04
react_rate = 0.3
deprotect_rate = 0.25


def one_hot(axis):
    place = lax.broadcasted_iota(jnp.int32, (COLS, COLS), 1 - axis)
    column = lax.broadcasted_iota(jnp.int32, (COLS, COLS), axis)
    where_to = (place & 127) * TILES + (place >> 7)
    return jnp.where(where_to == column, 1.0, 0.0).astype(jnp.bfloat16)


def image_kernel(near_ref, mask_ref, w_ref, dill_ref, load_ref, out_ref, b_ref, i_ref):
    f32 = jnp.float32
    upper = lax.axis_index("src") < 2
    near, own = near_ref[...], mask_ref[...]
    band = jnp.concatenate([jnp.where(upper, near, own), jnp.where(upper, own, near)], axis=0)
    band = jnp.dot(band.astype(f32).astype(jnp.bfloat16), one_hot(0), preferred_element_type=f32)
    filled = 2 * HALF * KS
    b_ref[:, filled:, :] = jnp.zeros((TILES, b_ref.shape[1] - filled, 128), f32)
    lane = lax.broadcasted_iota(jnp.int32, (2 * HALF, 128), 1)
    moved = {}
    for m in range(-8, 12):
        tile, by = m % TILES, m // TILES
        block = band[:, 128 * tile : 128 * tile + 128]
        if by:
            block = pltpu.roll(block, (-by) % 128, 1)
            block = jnp.where((lane + by >= 0) & (lane + by < 128), block, 0.0)
        moved[m] = block
    for b in range(KS):
        for t in range(TILES):
            b_ref[t, pl.ds(b, 2 * HALF, stride=KS), :] = moved[t + b - 8]
    w_all = w_ref[...].reshape(384, WLANES)
    weight = w_all[:, WCOL : WCOL + 1].astype(f32)
    w_taps = w_all[:, :KPAD]

    def body(q, carry):
        base = pl.multiple_of(q * (8 * KS), 8)
        view = b_ref.at[:, pl.ds(base, 424), :]
        for d in range(8):
            patches = jnp.concatenate(
                [view[t, KS * d : KS * d + KPAD, :] for t in range(TILES)], axis=1
            ).astype(jnp.bfloat16)
            field = jnp.dot(w_taps, patches, preferred_element_type=f32)
            power = (field * field * weight).reshape(4, 4, 3, 8, COLS)
            total = power.sum(axis=(0, 2)).sum(axis=1)
            for k in range(4):
                at = k * HALF + (d % 4) * 4 + d // 4 + 2 * q
                i_ref[pl.ds(at, 1), :] = total[k : k + 1]
        return carry

    lax.fori_loop(0, HALF // 8, body, 0)
    i_ref[PARAMS:, :] = jnp.zeros((16, COLS), f32)
    at = PARAMS
    for ref in (dill_ref, load_ref):
        for k in range(2):
            rest = jnp.full((1, COLS), ref[k], f32)
            for _ in range(3):
                part = rest.astype(jnp.bfloat16).astype(f32)
                i_ref[at : at + 1, :] = part
                rest = rest - part
                at += 1
    out_ref[...] = i_ref[...].astype(jnp.bfloat16)


def bake_kernel(scale, g_ref, acid_ref, inhib_ref, a_ref, q_ref, d_ref):
    f32 = jnp.float32
    tile = lax.axis_index("tile")
    src = lax.axis_index("src")
    lane = lax.broadcasted_iota(jnp.int32, (8, 128), 1)
    sub = lax.broadcasted_iota(jnp.int32, (8, 128), 0)
    has_up = jnp.where(tile > 0, 1.0, 0.0).astype(f32)
    has_down = jnp.where(tile < lax.axis_size("tile") - 1, 1.0, 0.0).astype(f32)
    keep = jnp.where(sub < 2, has_up, jnp.where(sub >= 6, has_down, 1.0))
    top = sub < 4
    for k in range(PLANES):
        par = g_ref[k // 2, PARAMS : PARAMS + 16, 0:128].astype(f32)

        def constant(at):
            return jnp.broadcast_to(par[at : at + 1] + par[at + 1 : at + 2] + par[at + 2 : at + 3], (8, 128))

        dill = constant(3 * (k % 2)) * -scale
        load = constant(6 + 3 * (k % 2)) * keep
        first = (k % 4) * HALF
        for t in range(TILES):
            cut = slice(128 * t, 128 * t + 128)
            high = g_ref[k // 4, first : first + HALF, cut].astype(f32)
            low = g_ref[k // 4 + 2, first : first + HALF, cut].astype(f32)
            for half in range(2):
                one, two = high[8 * half : 8 * half + 8], low[8 * half : 8 * half + 8]
                pair = (jnp.where(top, one, pltpu.roll(two, 4, 0)), jnp.where(top, pltpu.roll(one, 4, 0), two))
                for i in range(2):
                    at = (2 * half + i) * TILES + t
                    a_ref[0, k, at] = (1.0 - jnp.exp(dill * pair[i])) * keep
                    q_ref[0, k, at] = load

    not_first, not_last = lane > 0, lane < 127
    acid_keep = keep * (1.0 - 4.0 * acid_lateral - 2.0 * acid_vertical)
    load_keep = keep * (1.0 - 4.0 * quench_lateral - 2.0 * quench_vertical)
    acid_side, acid_up = keep * acid_lateral, keep * acid_vertical
    load_side, load_up = keep * quench_lateral, keep * quench_vertical
    react = keep * react_rate

    def around(ref, now, k, here):
        under, over = jnp.maximum(k - 1, 0), jnp.minimum(k + 1, PLANES - 1)
        side, vertical = [], []
        for u in range(GROUPS):
            for t in range(TILES):
                at = u * TILES + t
                above = here[at - TILES] if u > 0 else pltpu.roll(here[at + 3 * TILES], 1, 0)
                below = here[at + TILES] if u < GROUPS - 1 else pltpu.roll(here[at - 3 * TILES], 7, 0)
                left = here[at - 1] if t > 0 else jnp.where(not_first, pltpu.roll(here[at + 3], 1, 1), 0.0)
                right = here[at + 1] if t < TILES - 1 else jnp.where(not_last, pltpu.roll(here[at - 3], 127, 1), 0.0)
                side.append((above + below) + (left + right))
                vertical.append(ref[now, under, at] + ref[now, over, at])
        return side, vertical

    for step in range(STEPS):
        now, later = step % 2, (step + 1) % 2
        reach = STEPS - 1 - step

        def body(k, carry):
            acid = [a_ref[now, k, at] for at in range(16)]
            load = [q_ref[now, k, at] for at in range(16)]
            a_side, a_up = around(a_ref, now, k, acid)
            q_side, q_up = around(q_ref, now, k, load)
            for at in range(16):
                reacted = (react * acid[at]) * load[at]
                a_ref[later, k, at] = (acid_keep * acid[at] + acid_side * a_side[at]) + (acid_up * a_up[at] - reacted)
                q_ref[later, k, at] = (load_keep * load[at] + load_side * q_side[at]) + (load_up * q_up[at] - reacted)
            return carry

        lax.fori_loop(jnp.maximum(2 * src - reach, 0), jnp.minimum(2 * src + 1 + reach, PLANES - 1) + 1, body, 0)
        for k in range(2):
            for at in range(16):
                value = a_ref[later, 2 * src + k, at]
                d_ref[k, at] = value if step == 0 else d_ref[k, at] + value

    end = STEPS % 2
    blocks = []
    for k in range(2):
        for u in range(GROUPS):
            blocks.append(jnp.concatenate([a_ref[end, 2 * src + k, u * TILES + t] for t in range(TILES)], axis=1))
    for k in range(2):
        for u in range(GROUPS):
            blocks.append(jnp.concatenate([d_ref[k, u * TILES + t] for t in range(TILES)], axis=1))
    rest = jnp.concatenate(blocks, axis=0)
    back = one_hot(1)
    result = None
    for _ in range(3):
        part = rest.astype(jnp.bfloat16)
        rest = rest - part.astype(f32)
        moved = jnp.dot(part, back, preferred_element_type=f32)
        result = moved if result is None else result + moved
    inhibitor = jnp.exp(-deprotect_rate * result[64:])
    for k in range(2):
        for u in range(GROUPS):
            for j in range(2, 6):
                row = 32 * k + 8 * u + j
                to = 4 * (j - 2) + u
                acid_ref[k, to : to + 1, :] = result[row : row + 1]
                inhib_ref[k, to : to + 1, :] = inhibitor[row : row + 1]


def shards(mask_tiles, kernels, source_weight, dill_rate, quencher_load):
    bf16 = jnp.bfloat16
    tiles, parts = lax.axis_size("tile"), lax.axis_size("src")
    sources = kernels.shape[0]
    moves = []
    for i in range(tiles - 1):
        for s in range(parts):
            one, two = i * parts + s, (i + 1) * parts + s
            moves.append((one, two) if s < 2 else (two, one))
    near = lax.ppermute(mask_tiles, ("tile", "src"), moves)

    taps = kernels.reshape(sources, 3, 2, 4, 2, KS, KS).transpose(2, 3, 0, 1, 4, 5, 6).reshape(2, 96, TAPS)
    weight = jnp.broadcast_to(source_weight.astype(bf16)[None, None, :, None], (2, 4, sources, 6)).reshape(2, 96, 1)
    packed = jnp.concatenate(
        [taps, jnp.zeros((2, 96, WCOL - TAPS), bf16), weight, jnp.zeros((2, 96, WLANES - WCOL - 1), bf16)], axis=2
    )
    w_own = lax.all_to_all(jnp.concatenate([packed, packed], axis=0), "src", 0, 0)

    smem = pl.BlockSpec(memory_space=pltpu.SMEM)
    vmem = pl.BlockSpec(memory_space=pltpu.VMEM)
    intensity = pl.pallas_call(
        image_kernel,
        out_shape=jax.ShapeDtypeStruct((PARAMS + 16, COLS), bf16),
        in_specs=[vmem, vmem, vmem, smem, smem],
        scratch_shapes=[
            pltpu.VMEM((TILES, 560, 128), jnp.float32),
            pltpu.VMEM((PARAMS + 16, COLS), jnp.float32),
        ],
        compiler_params=pltpu.CompilerParams(vmem_limit_bytes=32 * 1024 * 1024),
        name="image",
    )(near, mask_tiles, w_own, dill_rate, quencher_load)
    gathered = lax.all_gather(intensity, "src")
    scale = 1.0 / (24.0 * sources * parts)

    def bake(*refs):
        bake_kernel(scale, *refs)

    out = jax.ShapeDtypeStruct((2, OWN, COLS), jnp.float32)
    acid, inhibitor = pl.pallas_call(
        bake,
        out_shape=(out, out),
        scratch_shapes=[
            pltpu.VMEM((2, PLANES, 16, 8, 128), jnp.float32),
            pltpu.VMEM((2, PLANES, 16, 8, 128), jnp.float32),
            pltpu.VMEM((2, 16, 8, 128), jnp.float32),
        ],
        compiler_params=pltpu.CompilerParams(vmem_limit_bytes=32 * 1024 * 1024),
        name="bake",
    )(gathered)
    return acid, inhibitor


def solution(mesh):
    in_specs = (
        P("tile", None),
        P("src", None, None, None, None, None),
        P("src"),
        P("src"),
        P("src"),
    )
    out_specs = (P("src", "tile", None), P("src", "tile", None))
    return jax.shard_map(shards, mesh=mesh, in_specs=in_specs, out_specs=out_specs, check_vma=False)
```

time: 49.5 us -> 40.9 us (0.83)
  starting transfers between devices: 19.5 us -> 10.1 us
  waiting for transfers between devices: 1 us -> 9.3 us
  Pallas kernels: 15.9 us -> 10.8 us
  local copies, waits for them, and re-layouts: 3.77 us -> 2.24 us
    ppermute x2 -> x1, starting transfers between devices: 15.2 us -> 5.8 us  [shards(): near = lax.ppermute(mask_tiles, ('tile', 'src'), moves)]
    ppermute x2 -> x1, waiting for transfers between devices: 0.99 us -> 9.3 us  [shards(): near = lax.ppermute(mask_tiles, ('tile', 'src'), moves)]
    pallas_call x1, Pallas kernels: 10.9 us -> 6.15 us  [shards(): pl.pallas_call(bake, out_shape=(out, out), scratch_shapes=[pltpu.VMEM((2,...]
    another operation x2 -> x0, other arithmetic: 1.32 us -> none  [shards(): values = jnp.stack(pieces(dill_rate) + pieces(quencher_load), axis=1)]
    concatenate x0 -> x1, other arithmetic: none -> 0.86 us  [shards(): jnp.concatenate([packed, packed], axis=0)]
    concatenate x1 -> x0, local copies, waits for them, and re-layouts: 0.8 us -> none  [shards(): jnp.concatenate([taps, jnp.zeros((4, 48, WCOL - TAPS), bf16), weight, val...]
    another operation x7 -> x0, local copies, waits for them, and re-layouts: 0.74 us -> none  [shards(): values = jnp.stack(pieces(dill_rate) + pieces(quencher_load), axis=1)]
  transfers between devices with their start and end apart: 3 -> 2, of which waited for: 1 -> 1; matrix products, arithmetic and copies ran while one was open for 0% -> 0% of each run, Pallas kernels for 0% -> 0%
where the time goes in v1:
time: 40.9 us; the launch traced here: 40.7 us
  Pallas kernels  10.8 us (26%)
  starting transfers between devices  10.1 us (25%)
  waiting for transfers between devices  9.3 us (23%)
  blocking collectives  6.64 us (16%)
  local copies, waits for them, and re-layouts  2.24 us (5%)
  other arithmetic  0.86 us (2%)
  between operations  0.73 us (2%)
    ppermute x1, waiting for transfers between devices, shards(): near = lax.ppermute(mask_tiles, ('tile', 'src'), moves)  9.3 us
    all_gather x1, blocking collectives, shards(): gathered = lax.all_gather(intensity, 'src')  6.64 us
    pallas_call x1, Pallas kernels, shards(): pl.pallas_call(bake, out_shape=(out, out), scratch_shapes=[pltpu.VMEM((2,...  6.15 us
    ppermute x1, starting transfers between devices, shards(): near = lax.ppermute(mask_tiles, ('tile', 'src'), moves)  5.8 us
    pallas_call x1, Pallas kernels, shards(): pl.pallas_call(image_kernel, out_shape=jax.ShapeDtypeStruct((PARAMS + 16,...  4.64 us
    all_to_all x1, starting transfers between devices, shards(): lax.all_to_all(jnp.concatenate([packed, packed], axis=0), 'src', 0, 0)  4.31 us
    reshape x2, local copies, waits for them, and re-layouts, shards(): kernels.reshape(sources, 3, 2, 4, 2, KS, KS).transpose(2, 3, 0, 1, 4, 5, 6)  1.94 us
    concatenate x1, other arithmetic, shards(): jnp.concatenate([packed, packed], axis=0)  0.86 us
  transfers between devices with their start and end apart: 2, of which 1 were waited for; matrix products, arithmetic and copies ran while one was open for 0% of the time, Pallas kernels for 0%

profile of v1, /device:TPU:49, one launch (start us, length us, event | category | flops | bytes accessed | tf_op | source)
XLA Modules:
  0.0 40.7 jit_solution(17584863679636888154)
XLA Ops:
  0.6 0.0 copy-start.3
  0.6 1.4 %copy.10 = bf16[4,3,2,4,2,17,17]{6,5,4,1,0,3,2:T(8,128)(2,1)S(1)} copy(bf16[4,3,2,4,2,17,17]{6,4,5,3,2,1,0:T(2,128)(2,1)} %bitcast.7) | data formatting | bytes 221952 | tf_op jit(solution)/shard_map/reshape | solution.py:201
  2.0 0.0 copy-start
  2.0 0.0 copy-start.1
  2.0 0.0 copy-start.2
  2.1 0.6 %reshape.14 = bf16[2,96,289]{2,1,0:T(8,128)(2,1)S(1)} reshape(bf16[2,4,4,3,2,17,17]{6,5,4,3,2,1,0:T(8,128)(2,1)S(1)} %bitcast.6) | data formatting | bytes 221952 | tf_op jit(solution)/shard_map/reshape | solution.py:201
  2.6 0.0 copy-done.3
  2.7 0.1 broadcast_in_dim.17
  2.7 0.1 broadcast_in_dim.18
  2.8 0.1 broadcast_in_dim.19
  2.9 0.9 %maximum_maximum_fusion = bf16[4,96,384]{2,1,0:T(8,128)(2,1)} fusion(bf16[2,96,79]{2,1,0:T(8,128)(2,1)S(1)} %broadcast_in_dim.20, bf16[2,96,1]{2,1,0:T(8,128)(2,1)S(1)} %broadcast_in_dim.19, bf16[2,96,15]{2,1,0:T(8,128)(2,1)S(1)} %broadcast_in_dim.16, bf16[2,96,289]{2,1,0:T(8,128)(2,1)S(1)} %reshape.14), kind=kLoop, calls=%fused_computation.1 | loop fusion | flops 2359296 | bytes 442368 | tf_op jit(solution)/shard_map/concatenate | solution.py:206
  3.8 4.3 %all-to-all-start = ((bf16[4,96,384]{2,1,0:T(8,128)(2,1)}), bf16[4,96,384]{2,1,0:T(8,128)(2,1)S(1)}, u32[]{:S(2)}, u32[]{:S(2)}) async-start(bf16[4,96,384]{2,1,0:T(8,128)(2,1)} %maximum_maximum_fusion), calls=%async_computation | async-start | bytes 589824 | tf_op jit(solution)/shard_map/all_to_all | solution.py:206
  8.1 0.0 copy-done
  8.1 5.8 %collective-permute-start = (s32[16,512]{1,0:T(8,128)S(1)}, s32[16,512]{1,0:T(8,128)S(1)}, u32[]{:S(2)}, u32[]{:S(2)}) collective-permute-start(s32[16,512]{1,0:T(8,128)S(1)} %copy-done), channel_id=1, source_target_pairs={{0,4},{1,5},{6,2},{7,3},{4,8},{5,9},{10,6},{11,7},{8,12},{9,13},{1... | collective-permute-start | bytes 98312 | tf_op jit(solution)/shard_map/ppermute | solution.py:199
  13.9 9.3 %collective-permute-done.near_ref = s32[16,512]{1,0:T(8,128)S(1)} collective-permute-done((s32[16,512]{1,0:T(8,128)S(1)}, s32[16,512]{1,0:T(8,128)S(1)}, u32[]{:S(2)}, u32[]{:S(2)}) %collective-permute-start) | collective-permute-done | bytes 32800 | tf_op jit(solution)/shard_map/ppermute | solution.py:199
  23.2 0.0 all-to-all-done.w_ref
  23.2 0.0 copy-done.1
  23.2 0.0 copy-done.2
  23.2 4.6 %image.1 = bf16[80,512]{1,0:T(8,128)(2,1)S(1)} custom-call(s32[16,512]{1,0:T(8,128)S(1)} %collective-permute-done.near_ref, s32[16,512]{1,0:T(8,128)S(1)} %copy-done, bf16[4,96,384]{2,1,0:T(8,128)(2,1)S(1)} %all-to-all-done.w_ref, f32[2]{0:T(128)S(1)} %copy-done.1, f32[2]{0:T(128)S(1)} %copy-done.2), custom_call_target="tpu_custom_call" | custom-call | tf_op jit(solution)/shard_map/image/pallas_call | solution.py:210
  27.9 6.6 %all-gather = bf16[320,512]{1,0:T(8,128)(2,1)S(1)} all-gather(bf16[80,512]{1,0:T(8,128)(2,1)S(1)} %image.1), channel_id=2, replica_groups=mesh['tile'=128,'src'=4] {'src'}, dimensions={0}, use_global_device_ids=true | all-gather | bytes 409600 | tf_op jit(solution)/shard_map/all_gather | solution.py:221
  34.5 6.1 %bake.1 = (f32[2,16,512]{2,1,0:T(8,128)}, f32[2,16,512]{2,1,0:T(8,128)}) custom-call(bf16[4,80,512]{2,1,0:T(8,128)(2,1)S(1)} %bitcast.5), custom_call_target="tpu_custom_call" | custom-call | tf_op jit(solution)/shard_map/bake/pallas_call | solution.py:228
  (3 shorter events, 0.0 us)
Async XLA Ops:
  0.6 2.0 %copy-start.3 = (s32[4]{0:T(128)S(1)}, s32[4]{0:T(128)}, u32[]{:S(2)}) copy-start(s32[4]{0:T(128)} %param.7) | copy-start | bytes 52
  2.0 6.1 %copy-start = (s32[16,512]{1,0:T(8,128)S(1)}, s32[16,512]{1,0:T(8,128)}, u32[]{:S(2)}) copy-start(s32[16,512]{1,0:T(8,128)} %mask_ref.1) | copy-start | bytes 98308
  2.0 21.2 %copy-start.1 = (f32[2]{0:T(128)S(1)}, f32[2]{0:T(128)}, u32[]{:S(2)}) copy-start(f32[2]{0:T(128)} %dill_ref.1) | copy-start | bytes 28
  2.0 21.2 %copy-start.2 = (f32[2]{0:T(128)S(1)}, f32[2]{0:T(128)}, u32[]{:S(2)}) copy-start(f32[2]{0:T(128)} %load_ref.1) | copy-start | bytes 28
  3.8 19.4 %all-to-all-start = ((bf16[4,96,384]{2,1,0:T(8,128)(2,1)}), bf16[4,96,384]{2,1,0:T(8,128)(2,1)S(1)}, u32[]{:S(2)}, u32[]{:S(2)}) async-start(bf16[4,96,384]{2,1,0:T(8,128)(2,1)} %maximum_maximum_fusion), calls=%async_computation | async-start | bytes 589824 | tf_op jit(solution)/shard_map/all_to_all | solution.py:206
  8.1 15.1 %collective-permute-start = (s32[16,512]{1,0:T(8,128)S(1)}, s32[16,512]{1,0:T(8,128)S(1)}, u32[]{:S(2)}, u32[]{:S(2)}) collective-permute-start(s32[16,512]{1,0:T(8,128)S(1)} %copy-done), channel_id=1, source_target_pairs={{0,4},{1,5},{6,2},{7,3},{4,8},{5,9},{10,6},{11,7},{8,12},{9,13},{1... | collective-permute-start | bytes 98312 | tf_op jit(solution)/shard_map/ppermute | solution.py:199

commit v2 on v1

--- a/solution.py
+++ b/solution.py
@@ -33,6 +33,21 @@
     column = lax.broadcasted_iota(jnp.int32, (COLS, COLS), axis)
     where_to = (place & 127) * TILES + (place >> 7)
     return jnp.where(where_to == column, 1.0, 0.0).astype(jnp.bfloat16)
+
+
+def pack_kernel(taps_ref, weight_ref, out_ref):
+    row = lax.broadcasted_iota(jnp.int32, (96, 128), 0)
+    lane = lax.broadcasted_iota(jnp.int32, (96, 128), 1)
+    source = (row // 6) & 3
+    weight = jnp.zeros((96, 128), jnp.float32)
+    for p in range(4):
+        weight = jnp.where(source == p, weight_ref[p].astype(jnp.float32), weight)
+    tail = jnp.where(lane == WCOL - 256, weight, 0.0).astype(jnp.bfloat16)
+    for half in range(2):
+        last = jnp.concatenate([taps_ref[half, :, 256:], tail[:, TAPS - 256 :]], axis=1)
+        for part in (half, half + 2):
+            out_ref[part, :, :256] = taps_ref[half, :, :256]
+            out_ref[part, :, 256:] = last
 
 
 def image_kernel(near_ref, mask_ref, w_ref, dill_ref, load_ref, out_ref, b_ref, i_ref):
@@ -88,7 +103,7 @@
     out_ref[...] = i_ref[...].astype(jnp.bfloat16)
 
 
-def bake_kernel(scale, g_ref, acid_ref, inhib_ref, a_ref, q_ref, d_ref):
+def bake_kernel(scale, g_ref, acid_ref, inhib_ref, a0_ref, a1_ref, q0_ref, q1_ref, d_ref):
     f32 = jnp.float32
     tile = lax.axis_index("tile")
     src = lax.axis_index("src")
@@ -98,6 +113,7 @@
     has_down = jnp.where(tile < lax.axis_size("tile") - 1, 1.0, 0.0).astype(f32)
     keep = jnp.where(sub < 2, has_up, jnp.where(sub >= 6, has_down, 1.0))
     top = sub < 4
+    scaled = keep * react_rate
     for k in range(PLANES):
         par = g_ref[k // 2, PARAMS : PARAMS + 16, 0:128].astype(f32)
 
@@ -105,7 +121,7 @@
             return jnp.broadcast_to(par[at : at + 1] + par[at + 1 : at + 2] + par[at + 2 : at + 3], (8, 128))
 
         dill = constant(3 * (k % 2)) * -scale
-        load = constant(6 + 3 * (k % 2)) * keep
+        load = constant(6 + 3 * (k % 2)) * scaled
         first = (k % 4) * HALF
         for t in range(TILES):
             cut = slice(128 * t, 128 * t + 128)
@@ -116,17 +132,16 @@
                 pair = (jnp.where(top, one, pltpu.roll(two, 4, 0)), jnp.where(top, pltpu.roll(one, 4, 0), two))
                 for i in range(2):
                     at = (2 * half + i) * TILES + t
-                    a_ref[0, k, at] = (1.0 - jnp.exp(dill * pair[i])) * keep
-                    q_ref[0, k, at] = load
+                    a0_ref[k, at] = (1.0 - jnp.exp(dill * pair[i])) * scaled
+                    q0_ref[k, at] = load
 
     not_first, not_last = lane > 0, lane < 127
     acid_keep = keep * (1.0 - 4.0 * acid_lateral - 2.0 * acid_vertical)
     load_keep = keep * (1.0 - 4.0 * quench_lateral - 2.0 * quench_vertical)
     acid_side, acid_up = keep * acid_lateral, keep * acid_vertical
     load_side, load_up = keep * quench_lateral, keep * quench_vertical
-    react = keep * react_rate
-
-    def around(ref, now, k, here):
+
+    def around(ref, k, here):
         under, over = jnp.maximum(k - 1, 0), jnp.minimum(k + 1, PLANES - 1)
         side, vertical = [], []
         for u in range(GROUPS):
@@ -137,35 +152,43 @@
                 left = here[at - 1] if t > 0 else jnp.where(not_first, pltpu.roll(here[at + 3], 1, 1), 0.0)
                 right = here[at + 1] if t < TILES - 1 else jnp.where(not_last, pltpu.roll(here[at - 3], 127, 1), 0.0)
                 side.append((above + below) + (left + right))
-                vertical.append(ref[now, under, at] + ref[now, over, at])
+                vertical.append(ref[under, at] + ref[over, at])
         return side, vertical
 
     for step in range(STEPS):
-        now, later = step % 2, (step + 1) % 2
+        a_now, a_new = (a0_ref, a1_ref) if step % 2 == 0 else (a1_ref, a0_ref)
+        q_now, q_new = (q0_ref, q1_ref) if step % 2 == 0 else (q1_ref, q0_ref)
         reach = STEPS - 1 - step
 
-        def body(k, carry):
-            acid = [a_ref[now, k, at] for at in range(16)]
-            load = [q_ref[now, k, at] for at in range(16)]
-            a_side, a_up = around(a_ref, now, k, acid)
-            q_side, q_up = around(q_ref, now, k, load)
+        low = jnp.maximum(2 * src - reach, 0)
+        count = (jnp.minimum(2 * src + 1 + reach, PLANES - 1) + 2 - low) // 2
+        low = jnp.minimum(low, PLANES - 2 * count)
+
+        def body(i, carry):
+            for j in range(2):
+                plane(low + 2 * i + j)
+            return carry
+
+        def plane(k):
+            acid = [a_now[k, at] for at in range(16)]
+            load = [q_now[k, at] for at in range(16)]
+            a_side, a_up = around(a_now, k, acid)
+            q_side, q_up = around(q_now, k, load)
             for at in range(16):
-                reacted = (react * acid[at]) * load[at]
-                a_ref[later, k, at] = (acid_keep * acid[at] + acid_side * a_side[at]) + (acid_up * a_up[at] - reacted)
-                q_ref[later, k, at] = (load_keep * load[at] + load_side * q_side[at]) + (load_up * q_up[at] - reacted)
-            return carry
-
-        lax.fori_loop(jnp.maximum(2 * src - reach, 0), jnp.minimum(2 * src + 1 + reach, PLANES - 1) + 1, body, 0)
+                reacted = acid[at] * load[at]
+                a_new[k, at] = (acid_keep * acid[at] + acid_side * a_side[at]) + (acid_up * a_up[at] - reacted)
+                q_new[k, at] = (load_keep * load[at] + load_side * q_side[at]) + (load_up * q_up[at] - reacted)
+
+        lax.fori_loop(0, count, body, 0)
         for k in range(2):
             for at in range(16):
-                value = a_ref[later, 2 * src + k, at]
+                value = a_new[2 * src + k, at]
                 d_ref[k, at] = value if step == 0 else d_ref[k, at] + value
 
-    end = STEPS % 2
     blocks = []
     for k in range(2):
         for u in range(GROUPS):
-            blocks.append(jnp.concatenate([a_ref[end, 2 * src + k, u * TILES + t] for t in range(TILES)], axis=1))
+            blocks.append(jnp.concatenate([a_new[2 * src + k, u * TILES + t] for t in range(TILES)], axis=1))
     for k in range(2):
         for u in range(GROUPS):
             blocks.append(jnp.concatenate([d_ref[k, u * TILES + t] for t in range(TILES)], axis=1))
@@ -177,15 +200,20 @@
         rest = rest - part.astype(f32)
         moved = jnp.dot(part, back, preferred_element_type=f32)
         result = moved if result is None else result + moved
-    inhibitor = jnp.exp(-deprotect_rate * result[64:])
+    inhibitor = jnp.exp((-deprotect_rate / react_rate) * result[64:])
+    acid_out = result[:64] * (1.0 / react_rate)
     for k in range(2):
         for u in range(GROUPS):
             for j in range(2, 6):
                 row = 32 * k + 8 * u + j
                 to = 4 * (j - 2) + u
-                acid_ref[k, to : to + 1, :] = result[row : row + 1]
+                acid_ref[k, to : to + 1, :] = acid_out[row : row + 1]
                 inhib_ref[k, to : to + 1, :] = inhibitor[row : row + 1]
 
+
+def bake_scratch():
+    state = pltpu.VMEM((PLANES, 16, 8, 128), jnp.float32)
+    return [state, state, state, state, pltpu.VMEM((2, 16, 8, 128), jnp.float32)]
 
 def shards(mask_tiles, kernels, source_weight, dill_rate, quencher_load):
     bf16 = jnp.bfloat16
@@ -199,14 +227,18 @@
     near = lax.ppermute(mask_tiles, ("tile", "src"), moves)
 
     taps = kernels.reshape(sources, 3, 2, 4, 2, KS, KS).transpose(2, 3, 0, 1, 4, 5, 6).reshape(2, 96, TAPS)
-    weight = jnp.broadcast_to(source_weight.astype(bf16)[None, None, :, None], (2, 4, sources, 6)).reshape(2, 96, 1)
-    packed = jnp.concatenate(
-        [taps, jnp.zeros((2, 96, WCOL - TAPS), bf16), weight, jnp.zeros((2, 96, WLANES - WCOL - 1), bf16)], axis=2
-    )
-    w_own = lax.all_to_all(jnp.concatenate([packed, packed], axis=0), "src", 0, 0)
-
     smem = pl.BlockSpec(memory_space=pltpu.SMEM)
     vmem = pl.BlockSpec(memory_space=pltpu.VMEM)
+    packed = pl.pallas_call(
+        pack_kernel,
+        out_shape=jax.ShapeDtypeStruct((parts, 96, WLANES), bf16),
+        in_specs=[vmem, smem],
+        out_specs=vmem,
+        compiler_params=pltpu.CompilerParams(vmem_limit_bytes=16 * 1024 * 1024),
+        name="pack",
+    )(taps, source_weight)
+    w_own = lax.all_to_all(packed, "src", 0, 0)
+
     intensity = pl.pallas_call(
         image_kernel,
         out_shape=jax.ShapeDtypeStruct((PARAMS + 16, COLS), bf16),
@@ -215,7 +247,7 @@
             pltpu.VMEM((TILES, 560, 128), jnp.float32),
             pltpu.VMEM((PARAMS + 16, COLS), jnp.float32),
         ],
-        compiler_params=pltpu.CompilerParams(vmem_limit_bytes=32 * 1024 * 1024),
+        compiler_params=pltpu.CompilerParams(vmem_limit_bytes=16 * 1024 * 1024),
         name="image",
     )(near, mask_tiles, w_own, dill_rate, quencher_load)
     gathered = lax.all_gather(intensity, "src")
@@ -228,12 +260,8 @@
     acid, inhibitor = pl.pallas_call(
         bake,
         out_shape=(out, out),
-        scratch_shapes=[
-            pltpu.VMEM((2, PLANES, 16, 8, 128), jnp.float32),
-            pltpu.VMEM((2, PLANES, 16, 8, 128), jnp.float32),
-            pltpu.VMEM((2, 16, 8, 128), jnp.float32),
-        ],
-        compiler_params=pltpu.CompilerParams(vmem_limit_bytes=32 * 1024 * 1024),
+        scratch_shapes=bake_scratch(),
+        compiler_params=pltpu.CompilerParams(vmem_limit_bytes=16 * 1024 * 1024),
         name="bake",
     )(gathered)
     return acid, inhibitor

time: 40.9 us -> 39.6 us (0.968)
  the two profiles are of different devices: /device:TPU:49 before, /device:TPU:41 now
where the time goes in v2:
time: 39.6 us; the launch traced here: 39.3 us
  Pallas kernels  10.6 us (27%)
  starting transfers between devices  10.1 us (26%)
  waiting for transfers between devices  9.3 us (23%)
  blocking collectives  6.64 us (17%)
  local copies, waits for them, and re-layouts  1.97 us (5%)
  between operations  0.7 us (2%)
    ppermute x1, waiting for transfers between devices, shards(): near = lax.ppermute(mask_tiles, ('tile', 'src'), moves)  9.3 us
    all_gather x1, blocking collectives, shards(): gathered = lax.all_gather(intensity, 'src')  6.64 us
    ppermute x1, starting transfers between devices, shards(): near = lax.ppermute(mask_tiles, ('tile', 'src'), moves)  5.8 us
    pallas_call x1, Pallas kernels, shards(): pl.pallas_call(bake, out_shape=(out, out), scratch_shapes=bake_scratch(),...  4.71 us
    pallas_call x1, Pallas kernels, shards(): pl.pallas_call(image_kernel, out_shape=jax.ShapeDtypeStruct((PARAMS + 16,...  4.64 us
    all_to_all x1, starting transfers between devices, shards(): w_own = lax.all_to_all(packed, 'src', 0, 0)  4.31 us
    reshape x2, local copies, waits for them, and re-layouts, shards(): kernels.reshape(sources, 3, 2, 4, 2, KS, KS).transpose(2, 3, 0, 1, 4, 5, 6)  1.94 us
    pallas_call x1, Pallas kernels, shards(): pl.pallas_call(pack_kernel, out_shape=jax.ShapeDtypeStruct((parts, 96, WL...  1.28 us
  transfers between devices with their start and end apart: 2, of which 1 were waited for; matrix products, arithmetic and copies ran while one was open for 0% of the time, Pallas kernels for 0%

profile of v2, /device:TPU:41, one launch (start us, length us, event | category | flops | bytes accessed | tf_op | source)
XLA Modules:
  0.0 39.3 jit_solution(5072794188446266558)
XLA Ops:
  0.6 0.0 copy-start.3
  0.6 1.4 %copy.10 = bf16[4,3,2,4,2,17,17]{6,5,4,1,0,3,2:T(8,128)(2,1)S(1)} copy(bf16[4,3,2,4,2,17,17]{6,4,5,3,2,1,0:T(2,128)(2,1)} %bitcast.7) | data formatting | bytes 221952 | tf_op jit(solution)/shard_map/reshape | solution.py:229
  2.0 0.0 copy-start
  2.0 0.0 copy-start.1
  2.0 0.0 copy-start.2
  2.1 0.6 %reshape.11.taps_ref = bf16[2,96,289]{2,1,0:T(8,128)(2,1)S(1)} reshape(bf16[2,4,4,3,2,17,17]{6,5,4,3,2,1,0:T(8,128)(2,1)S(1)} %bitcast.6) | data formatting | bytes 221952 | tf_op jit(solution)/shard_map/reshape | solution.py:229
  2.6 0.0 copy-done.3
  2.6 1.3 %pack.1 = bf16[4,96,384]{2,1,0:T(8,128)(2,1)} custom-call(bf16[2,96,289]{2,1,0:T(8,128)(2,1)S(1)} %reshape.11.taps_ref, s32[4]{0:T(128)S(1)} %copy-done.3), custom_call_target="tpu_custom_call" | custom-call | tf_op jit(solution)/shard_map/pack/pallas_call | solution.py:232
  3.9 4.3 %all-to-all-start = ((bf16[4,96,384]{2,1,0:T(8,128)(2,1)}), bf16[4,96,384]{2,1,0:T(8,128)(2,1)S(1)}, u32[]{:S(2)}, u32[]{:S(2)}) async-start(bf16[4,96,384]{2,1,0:T(8,128)(2,1)} %pack.1), calls=%async_computation | async-start | bytes 589824 | tf_op jit(solution)/shard_map/all_to_all | solution.py:240
  8.2 0.0 copy-done
  8.2 5.8 %collective-permute-start = (s32[16,512]{1,0:T(8,128)S(1)}, s32[16,512]{1,0:T(8,128)S(1)}, u32[]{:S(2)}, u32[]{:S(2)}) collective-permute-start(s32[16,512]{1,0:T(8,128)S(1)} %copy-done), channel_id=1, source_target_pairs={{0,4},{1,5},{6,2},{7,3},{4,8},{5,9},{10,6},{11,7},{8,12},{9,13},{1... | collective-permute-start | bytes 98312 | tf_op jit(solution)/shard_map/ppermute | solution.py:227
  14.0 9.3 %collective-permute-done.near_ref = s32[16,512]{1,0:T(8,128)S(1)} collective-permute-done((s32[16,512]{1,0:T(8,128)S(1)}, s32[16,512]{1,0:T(8,128)S(1)}, u32[]{:S(2)}, u32[]{:S(2)}) %collective-permute-start) | collective-permute-done | bytes 32800 | tf_op jit(solution)/shard_map/ppermute | solution.py:227
  23.3 0.0 all-to-all-done.w_ref
  23.3 0.0 copy-done.1
  23.4 0.0 copy-done.2
  23.4 4.6 %image.1 = bf16[80,512]{1,0:T(8,128)(2,1)S(1)} custom-call(s32[16,512]{1,0:T(8,128)S(1)} %collective-permute-done.near_ref, s32[16,512]{1,0:T(8,128)S(1)} %copy-done, bf16[4,96,384]{2,1,0:T(8,128)(2,1)S(1)} %all-to-all-done.w_ref, f32[2]{0:T(128)S(1)} %copy-done.1, f32[2]{0:T(128)S(1)} %copy-done.2), custom_call_target="tpu_custom_call" | custom-call | tf_op jit(solution)/shard_map/image/pallas_call | solution.py:242
  28.0 6.6 %all-gather = bf16[320,512]{1,0:T(8,128)(2,1)S(1)} all-gather(bf16[80,512]{1,0:T(8,128)(2,1)S(1)} %image.1), channel_id=2, replica_groups=mesh['tile'=128,'src'=4] {'src'}, dimensions={0}, use_global_device_ids=true | all-gather | bytes 409600 | tf_op jit(solution)/shard_map/all_gather | solution.py:253
  34.6 4.7 %bake.1 = (f32[2,16,512]{2,1,0:T(8,128)}, f32[2,16,512]{2,1,0:T(8,128)}) custom-call(bf16[4,80,512]{2,1,0:T(8,128)(2,1)S(1)} %bitcast.5), custom_call_target="tpu_custom_call" | custom-call | tf_op jit(solution)/shard_map/bake/pallas_call | solution.py:260
Async XLA Ops:
  0.6 2.0 %copy-start.3 = (s32[4]{0:T(128)S(1)}, s32[4]{0:T(128)}, u32[]{:S(2)}) copy-start(s32[4]{0:T(128)} %weight_ref.1) | copy-start | bytes 52
  2.0 6.2 %copy-start = (s32[16,512]{1,0:T(8,128)S(1)}, s32[16,512]{1,0:T(8,128)}, u32[]{:S(2)}) copy-start(s32[16,512]{1,0:T(8,128)} %mask_ref.1) | copy-start | bytes 98308
  2.0 21.3 %copy-start.1 = (f32[2]{0:T(128)S(1)}, f32[2]{0:T(128)}, u32[]{:S(2)}) copy-start(f32[2]{0:T(128)} %dill_ref.1) | copy-start | bytes 28
  2.0 21.3 %copy-start.2 = (f32[2]{0:T(128)S(1)}, f32[2]{0:T(128)}, u32[]{:S(2)}) copy-start(f32[2]{0:T(128)} %load_ref.1) | copy-start | bytes 28
  3.9 19.4 %all-to-all-start = ((bf16[4,96,384]{2,1,0:T(8,128)(2,1)}), bf16[4,96,384]{2,1,0:T(8,128)(2,1)S(1)}, u32[]{:S(2)}, u32[]{:S(2)}) async-start(bf16[4,96,384]{2,1,0:T(8,128)(2,1)} %pack.1), calls=%async_computation | async-start | bytes 589824 | tf_op jit(solution)/shard_map/all_to_all | solution.py:240
  8.2 15.1 %collective-permute-start = (s32[16,512]{1,0:T(8,128)S(1)}, s32[16,512]{1,0:T(8,128)S(1)}, u32[]{:S(2)}, u32[]{:S(2)}) collective-permute-start(s32[16,512]{1,0:T(8,128)S(1)} %copy-done), channel_id=1, source_target_pairs={{0,4},{1,5},{6,2},{7,3},{4,8},{5,9},{10,6},{11,7},{8,12},{9,13},{1... | collective-permute-start | bytes 98312 | tf_op jit(solution)/shard_map/ppermute | solution.py:227

commit v3 on v2

--- a/solution.py
+++ b/solution.py
@@ -33,21 +33,6 @@
     column = lax.broadcasted_iota(jnp.int32, (COLS, COLS), axis)
     where_to = (place & 127) * TILES + (place >> 7)
     return jnp.where(where_to == column, 1.0, 0.0).astype(jnp.bfloat16)
-
-
-def pack_kernel(taps_ref, weight_ref, out_ref):
-    row = lax.broadcasted_iota(jnp.int32, (96, 128), 0)
-    lane = lax.broadcasted_iota(jnp.int32, (96, 128), 1)
-    source = (row // 6) & 3
-    weight = jnp.zeros((96, 128), jnp.float32)
-    for p in range(4):
-        weight = jnp.where(source == p, weight_ref[p].astype(jnp.float32), weight)
-    tail = jnp.where(lane == WCOL - 256, weight, 0.0).astype(jnp.bfloat16)
-    for half in range(2):
-        last = jnp.concatenate([taps_ref[half, :, 256:], tail[:, TAPS - 256 :]], axis=1)
-        for part in (half, half + 2):
-            out_ref[part, :, :256] = taps_ref[half, :, :256]
-            out_ref[part, :, 256:] = last
 
 
 def image_kernel(near_ref, mask_ref, w_ref, dill_ref, load_ref, out_ref, b_ref, i_ref):
@@ -226,19 +211,18 @@
             moves.append((one, two) if s < 2 else (two, one))
     near = lax.ppermute(mask_tiles, ("tile", "src"), moves)
 
-    taps = kernels.reshape(sources, 3, 2, 4, 2, KS, KS).transpose(2, 3, 0, 1, 4, 5, 6).reshape(2, 96, TAPS)
+    shape = (KS, KS, WLANES)
+    tap = lax.broadcasted_iota(jnp.int32, shape, 0) * KS + lax.broadcasted_iota(jnp.int32, shape, 1)
+    places = (lax.broadcasted_iota(jnp.int32, shape, 2) == tap).astype(bf16)
+    split = kernels.reshape(sources, 3, 2, 4, 2, KS, KS)
+    taps = jnp.einsum("pchkqab,abj->hkpcqj", split, places, preferred_element_type=bf16)
+    behind = lax.broadcasted_iota(jnp.int32, (1, 1, 1, 1, 1, WLANES), 5) == WCOL
+    taps = taps + jnp.where(behind, source_weight.astype(bf16).reshape(1, 1, sources, 1, 1, 1), 0)
+    packed = jnp.broadcast_to(taps[None], (2,) + taps.shape).reshape(parts, 96, WLANES)
+    w_own = lax.all_to_all(packed, "src", 0, 0)
+
     smem = pl.BlockSpec(memory_space=pltpu.SMEM)
     vmem = pl.BlockSpec(memory_space=pltpu.VMEM)
-    packed = pl.pallas_call(
-        pack_kernel,
-        out_shape=jax.ShapeDtypeStruct((parts, 96, WLANES), bf16),
-        in_specs=[vmem, smem],
-        out_specs=vmem,
-        compiler_params=pltpu.CompilerParams(vmem_limit_bytes=16 * 1024 * 1024),
-        name="pack",
-    )(taps, source_weight)
-    w_own = lax.all_to_all(packed, "src", 0, 0)
-
     intensity = pl.pallas_call(
         image_kernel,
         out_shape=jax.ShapeDtypeStruct((PARAMS + 16, COLS), bf16),

time: 39.6 us -> 39.5 us (level)
  the two profiles are of different devices: /device:TPU:41 before, /device:TPU:49 now
where the time goes in v3:
time: 39.5 us; the launch traced here: 39.3 us
  starting transfers between devices  10.2 us (26%)
  Pallas kernels  9.34 us (24%)
  waiting for transfers between devices  9.3 us (24%)
  blocking collectives  6.64 us (17%)
  local copies, waits for them, and re-layouts  2.15 us (5%)
  matrix products  0.78 us (2%)
  between operations  0.7 us (2%)
    ppermute x1, waiting for transfers between devices, shards(): near = lax.ppermute(mask_tiles, ('tile', 'src'), moves)  9.3 us
    all_gather x1, blocking collectives, shards(): gathered = lax.all_gather(intensity, 'src')  6.64 us
    ppermute x1, starting transfers between devices, shards(): near = lax.ppermute(mask_tiles, ('tile', 'src'), moves)  5.8 us
    pallas_call x1, Pallas kernels, shards(): pl.pallas_call(bake, out_shape=(out, out), scratch_shapes=bake_scratch(),...  4.71 us
    pallas_call x1, Pallas kernels, shards(): pl.pallas_call(image_kernel, out_shape=jax.ShapeDtypeStruct((PARAMS + 16,...  4.64 us
    all_to_all x1, starting transfers between devices, shards(): w_own = lax.all_to_all(packed, 'src', 0, 0)  4.44 us
    unnamed x10, local copies, waits for them, and re-layouts  1.06 us
    reshape x1, local copies, waits for them, and re-layouts, shards(): jnp.broadcast_to(taps[None], (2,) + taps.shape).reshape(parts, 96, WLANES)  0.82 us
  transfers between devices with their start and end apart: 2, of which 1 were waited for; matrix products, arithmetic and copies ran while one was open for 0% of the time, Pallas kernels for 0%

profile of v3, /device:TPU:49, one launch (start us, length us, event | category | flops | bytes accessed | tf_op | source)
XLA Modules:
  0.0 39.3 jit_solution(4726152463459044311)
XLA Ops:
  0.6 0.0 copy-start
  0.7 0.0 copy-start.4
  0.7 0.7 %copy-done.4 = s32[4]{0:T(128)S(1)} copy-done((s32[4]{0:T(128)S(1)}, s32[4]{0:T(128)}, u32[]{:S(2)}) %copy-start.4) | copy-done | bytes 40
  1.4 0.1 broadcast_select_fusion
  1.5 0.3 copy-done
  1.8 0.8 %fusion = bf16[2,4,4,3,2,384]{5,1,4,0,3,2:T(4,128)(2,1)S(1)} fusion(bf16[4,3,2,4,2,17,17]{6,4,5,3,2,1,0:T(2,128)(2,1)S(1)} %bitcast.14, s32[17]{0:T(128)S(1)} %iota_multiply_fusion, bf16[4,384]{1,0:T(4,128)(2,1)S(1)} %broadcast_select_fusion), kind=kOutput, calls=%fused_computation.1 | convolution fusion | flops 42910464 | bytes 261572 | tf_op jit(solution)/shard_map/pchkqab,abj->hkpcqj/dot_general | solution.py:218
  2.6 0.1 copy.8
  2.7 0.2 broadcast_in_dim.29
  2.9 0.8 %reshape.50 = bf16[4,96,384]{2,1,0:T(8,128)(2,1)} reshape(bf16[2,2,4,4,3,2,384]{6,5,4,3,2,1,0:T(2,128)(2,1)S(1)} %broadcast_in_dim.29) | data formatting | bytes 589824 | tf_op jit(solution)/shard_map/reshape | solution.py:221
  3.7 0.0 copy-start.1
  3.7 0.0 copy-start.2
  3.7 0.0 copy-start.3
  3.7 4.4 %all-to-all-start = ((bf16[4,96,384]{2,1,0:T(8,128)(2,1)}), bf16[4,96,384]{2,1,0:T(8,128)(2,1)S(1)}, u32[]{:S(2)}, u32[]{:S(2)}) async-start(bf16[4,96,384]{2,1,0:T(8,128)(2,1)} %reshape.50), calls=%async_computation | async-start | bytes 589824 | tf_op jit(solution)/shard_map/all_to_all | solution.py:222
  8.1 0.0 copy-done.1
  8.1 5.8 %collective-permute-start = (s32[16,512]{1,0:T(8,128)S(1)}, s32[16,512]{1,0:T(8,128)S(1)}, u32[]{:S(2)}, u32[]{:S(2)}) collective-permute-start(s32[16,512]{1,0:T(8,128)S(1)} %copy-done.1), channel_id=1, source_target_pairs={{0,4},{1,5},{6,2},{7,3},{4,8},{5,9},{10,6},{11,7},{8,12},{9,13},{1... | collective-permute-start | bytes 98312 | tf_op jit(solution)/shard_map/ppermute | solution.py:212
  14.0 9.3 %collective-permute-done.near_ref = s32[16,512]{1,0:T(8,128)S(1)} collective-permute-done((s32[16,512]{1,0:T(8,128)S(1)}, s32[16,512]{1,0:T(8,128)S(1)}, u32[]{:S(2)}, u32[]{:S(2)}) %collective-permute-start) | collective-permute-done | bytes 32800 | tf_op jit(solution)/shard_map/ppermute | solution.py:212
  23.3 0.0 all-to-all-done.w_ref
  23.3 0.0 copy-done.2
  23.3 0.0 copy-done.3
  23.3 4.6 %image.1 = bf16[80,512]{1,0:T(8,128)(2,1)S(1)} custom-call(s32[16,512]{1,0:T(8,128)S(1)} %collective-permute-done.near_ref, s32[16,512]{1,0:T(8,128)S(1)} %copy-done.1, bf16[4,96,384]{2,1,0:T(8,128)(2,1)S(1)} %all-to-all-done.w_ref, f32[2]{0:T(128)S(1)} %copy-done.2, f32[2]{0:T(128)S(1)} %copy-done.3), custom_call_target="tpu_custom_call" | custom-call | tf_op jit(solution)/shard_map/image/pallas_call | solution.py:226
  27.9 6.6 %all-gather = bf16[320,512]{1,0:T(8,128)(2,1)S(1)} all-gather(bf16[80,512]{1,0:T(8,128)(2,1)S(1)} %image.1), channel_id=2, replica_groups=mesh['tile'=128,'src'=4] {'src'}, dimensions={0}, use_global_device_ids=true | all-gather | bytes 409600 | tf_op jit(solution)/shard_map/all_gather | solution.py:237
  34.5 4.7 %bake.1 = (f32[2,16,512]{2,1,0:T(8,128)}, f32[2,16,512]{2,1,0:T(8,128)}) custom-call(bf16[4,80,512]{2,1,0:T(8,128)(2,1)S(1)} %bitcast.15), custom_call_target="tpu_custom_call" | custom-call | tf_op jit(solution)/shard_map/bake/pallas_call | solution.py:244
  (3 shorter events, 0.0 us)
Async XLA Ops:
  0.6 1.2 %copy-start = (bf16[4,3,8,2,17,17]{5,3,4,2,1,0:T(2,128)(2,1)S(1)}, bf16[4,3,8,2,17,17]{5,3,4,2,1,0:T(2,128)(2,1)}, u32[]{:S(2)}) copy-start(bf16[4,3,8,2,17,17]{5,3,4,2,1,0:T(2,128)(2,1)} %param.6) | copy-start | bytes 332932
  0.7 0.7 %copy-start.4 = (s32[4]{0:T(128)S(1)}, s32[4]{0:T(128)}, u32[]{:S(2)}) copy-start(s32[4]{0:T(128)} %param.7) | copy-start | bytes 52
  3.7 4.5 %copy-start.1 = (s32[16,512]{1,0:T(8,128)S(1)}, s32[16,512]{1,0:T(8,128)}, u32[]{:S(2)}) copy-start(s32[16,512]{1,0:T(8,128)} %mask_ref.1) | copy-start | bytes 98308
  3.7 19.6 %copy-start.2 = (f32[2]{0:T(128)S(1)}, f32[2]{0:T(128)}, u32[]{:S(2)}) copy-start(f32[2]{0:T(128)} %dill_ref.1) | copy-start | bytes 28
  3.7 19.6 %copy-start.3 = (f32[2]{0:T(128)S(1)}, f32[2]{0:T(128)}, u32[]{:S(2)}) copy-start(f32[2]{0:T(128)} %load_ref.1) | copy-start | bytes 28
  3.7 19.6 %all-to-all-start = ((bf16[4,96,384]{2,1,0:T(8,128)(2,1)}), bf16[4,96,384]{2,1,0:T(8,128)(2,1)S(1)}, u32[]{:S(2)}, u32[]{:S(2)}) async-start(bf16[4,96,384]{2,1,0:T(8,128)(2,1)} %reshape.50), calls=%async_computation | async-start | bytes 589824 | tf_op jit(solution)/shard_map/all_to_all | solution.py:222
  8.1 15.1 %collective-permute-start = (s32[16,512]{1,0:T(8,128)S(1)}, s32[16,512]{1,0:T(8,128)S(1)}, u32[]{:S(2)}, u32[]{:S(2)}) collective-permute-start(s32[16,512]{1,0:T(8,128)S(1)} %copy-done.1), channel_id=1, source_target_pairs={{0,4},{1,5},{6,2},{7,3},{4,8},{5,9},{10,6},{11,7},{8,12},{9,13},{1... | collective-permute-start | bytes 98312 | tf_op jit(solution)/shard_map/ppermute | solution.py:212

commit v4 on v3

--- a/solution.py
+++ b/solution.py
@@ -19,6 +19,8 @@
 PLANES = 8
 GROUPS = 4
 PARAMS = 64
+BAND_FLOPS = 1 << 34
+BAND_BYTES = 1 << 26
 
 acid_lateral = 0.15
 acid_vertical = 0.12
@@ -35,7 +37,7 @@
     return jnp.where(where_to == column, 1.0, 0.0).astype(jnp.bfloat16)
 
 
-def image_kernel(near_ref, mask_ref, w_ref, dill_ref, load_ref, out_ref, b_ref, i_ref):
+def band_kernel(near_ref, mask_ref, b_ref):
     f32 = jnp.float32
     upper = lax.axis_index("src") < 2
     near, own = near_ref[...], mask_ref[...]
@@ -55,7 +57,14 @@
     for b in range(KS):
         for t in range(TILES):
             b_ref[t, pl.ds(b, 2 * HALF, stride=KS), :] = moved[t + b - 8]
-    w_all = w_ref[...].reshape(384, WLANES)
+
+
+def image_kernel(b_ref, *refs):
+    f32 = jnp.float32
+    own_ref, near_e, far_e, *late = refs[:6]
+    dill_ref, load_ref, out_ref, i_ref = refs[6:]
+    early = [near_e[...], far_e[0], far_e[1]]
+    w_all = jnp.concatenate([own_ref[...]] + [e + l[...] for e, l in zip(early, late)], axis=0)
     weight = w_all[:, WCOL : WCOL + 1].astype(f32)
     w_taps = w_all[:, :KPAD]
 
@@ -211,29 +220,52 @@
             moves.append((one, two) if s < 2 else (two, one))
     near = lax.ppermute(mask_tiles, ("tile", "src"), moves)
 
-    shape = (KS, KS, WLANES)
-    tap = lax.broadcasted_iota(jnp.int32, shape, 0) * KS + lax.broadcasted_iota(jnp.int32, shape, 1)
-    places = (lax.broadcasted_iota(jnp.int32, shape, 2) == tap).astype(bf16)
+    lane = lax.broadcasted_iota(jnp.int32, (KS, KS, WLANES), 2)
+    tap = lax.broadcasted_iota(jnp.int32, (KS, KS, WLANES), 0) * KS + lax.broadcasted_iota(jnp.int32, (KS, KS, WLANES), 1)
+    places = (lane == tap).astype(bf16)
     split = kernels.reshape(sources, 3, 2, 4, 2, KS, KS)
     taps = jnp.einsum("pchkqab,abj->hkpcqj", split, places, preferred_element_type=bf16)
     behind = lax.broadcasted_iota(jnp.int32, (1, 1, 1, 1, 1, WLANES), 5) == WCOL
     taps = taps + jnp.where(behind, source_weight.astype(bf16).reshape(1, 1, sources, 1, 1, 1), 0)
-    packed = jnp.broadcast_to(taps[None], (2,) + taps.shape).reshape(parts, 96, WLANES)
-    w_own = lax.all_to_all(packed, "src", 0, 0)
+    taps = taps.reshape(2, 96, WLANES)
+    odd = lax.axis_index("src") % 2 == 1
+    same = jnp.where(odd, taps[1], taps[0])
+    other = jnp.where(odd, taps[0], taps[1])
+
+    def swap(block, late, bit):
+        pairs = [
+            (i * parts + s, i * parts + (s ^ bit))
+            for i in range(tiles)
+            if (i % 4 >= 2) == late
+            for s in range(parts)
+        ]
+        return lax.ppermute(block, ("tile", "src"), pairs)
+
+    near_e = swap(other, False, 1)
+    far_e = swap(jnp.stack([same, near_e]), False, 2)
+    same_later, other_later, near_e, far_e = lax.optimization_barrier((same, other, near_e, far_e))
+    late = [swap(block, True, bit) for block, bit in ((other_later, 1), (same_later, 2), (other_later, 3))]
 
     smem = pl.BlockSpec(memory_space=pltpu.SMEM)
     vmem = pl.BlockSpec(memory_space=pltpu.VMEM)
+    band = pl.pallas_call(
+        band_kernel,
+        out_shape=jax.ShapeDtypeStruct((TILES, 560, 128), jnp.float32),
+        in_specs=[vmem, vmem],
+        out_specs=vmem,
+        compiler_params=pltpu.CompilerParams(vmem_limit_bytes=16 * 1024 * 1024),
+        cost_estimate=pl.CostEstimate(flops=BAND_FLOPS, bytes_accessed=BAND_BYTES, transcendentals=0),
+        name="band",
+    )(near, mask_tiles)
     intensity = pl.pallas_call(
         image_kernel,
         out_shape=jax.ShapeDtypeStruct((PARAMS + 16, COLS), bf16),
-        in_specs=[vmem, vmem, vmem, smem, smem],
-        scratch_shapes=[
-            pltpu.VMEM((TILES, 560, 128), jnp.float32),
-            pltpu.VMEM((PARAMS + 16, COLS), jnp.float32),
-        ],
+        in_specs=[vmem] * 7 + [smem, smem],
+        out_specs=vmem,
+        scratch_shapes=[pltpu.VMEM((PARAMS + 16, COLS), jnp.float32)],
         compiler_params=pltpu.CompilerParams(vmem_limit_bytes=16 * 1024 * 1024),
         name="image",
-    )(near, mask_tiles, w_own, dill_rate, quencher_load)
+    )(band, same, near_e, far_e, *late, dill_rate, quencher_load)
     gathered = lax.all_gather(intensity, "src")
     scale = 1.0 / (24.0 * sources * parts)
 

time: 39.5 us -> 38.7 us (0.980)
  the two profiles are of different devices: /device:TPU:49 before, /device:TPU:33 now
where the time goes in v4:
time: 38.7 us; the launch traced here: 38.4 us
  starting transfers between devices  14.4 us (37%)
  Pallas kernels  9.41 us (24%)
  blocking collectives  7.61 us (20%)
  waiting for transfers between devices  3.87 us (10%)
  other arithmetic  0.9 us (2%)
  between operations  0.87 us (2%)
  matrix products  0.78 us (2%)
  local copies, waits for them, and re-layouts  0.55 us (1%)
    ppermute x5, starting transfers between devices, swap(): return lax.ppermute(block, ('tile', 'src'), pairs)  8.58 us
    all_gather x1, blocking collectives, shards(): gathered = lax.all_gather(intensity, 'src')  7.61 us
    ppermute x1, starting transfers between devices, shards(): near = lax.ppermute(mask_tiles, ('tile', 'src'), moves)  5.81 us
    pallas_call x1, Pallas kernels, shards(): pl.pallas_call(bake, out_shape=(out, out), scratch_shapes=bake_scratch(),...  4.71 us
    pallas_call x1, Pallas kernels, shards(): pl.pallas_call(image_kernel, out_shape=jax.ShapeDtypeStruct((PARAMS + 16,...  4.36 us
    ppermute x1, waiting for transfers between devices, shards(): near = lax.ppermute(mask_tiles, ('tile', 'src'), moves)  3.08 us
    ppermute x5, waiting for transfers between devices, swap(): return lax.ppermute(block, ('tile', 'src'), pairs)  0.8 us
    dot_general x1, matrix products, shards(): jnp.einsum('pchkqab,abj->hkpcqj', split, places, preferred_element_type=b...  0.78 us
  transfers between devices with their start and end apart: 6, of which 2 were waited for; matrix products, arithmetic and copies ran while one was open for 0% of the time, Pallas kernels for 1%

profile of v4, /device:TPU:33, one launch (start us, length us, event | category | flops | bytes accessed | tf_op | source)
XLA Modules:
  0.0 38.4 jit_solution(14374958914866537568)
XLA Ops:
  0.6 0.0 copy-start
  0.7 0.7 %convert_element_type.6 = bf16[4]{0:T(256)(128)(2,1)S(1)} convert(s32[4]{0:T(128)} %param.7) | non-fusion elementwise | flops 4 | bytes 24 | tf_op jit(solution)/shard_map/convert_element_type | solution.py:229
  1.4 0.1 broadcast_select_fusion.2
  1.5 0.3 copy-done
  1.8 0.8 %fusion = bf16[2,4,4,3,2,384]{5,1,4,0,3,2:T(4,128)(2,1)S(1)} fusion(bf16[4,3,2,4,2,17,17]{6,4,5,3,2,1,0:T(2,128)(2,1)S(1)} %bitcast.15, s32[17]{0:T(128)S(1)} %iota_multiply_fusion, bf16[4,384]{1,0:T(4,128)(2,1)S(1)} %broadcast_select_fusion.2), kind=kOutput, calls=%fused_computation.1 | convolution fusion | flops 42910464 | bytes 261572 | tf_op jit(solution)/shard_map/pchkqab,abj->hkpcqj/dot_general | solution.py:227
  2.6 0.0 copy-start.3
  2.6 0.1 broadcast_select_fusion
  2.7 0.1 copy.9
  2.8 2.6 %collective-permute-start.1 = (bf16[96,384]{1,0:T(8,128)(2,1)S(1)}, bf16[96,384]{1,0:T(8,128)(2,1)S(1)}, u32[]{:S(2)}, u32[]{:S(2)}) collective-permute-start(bf16[96,384]{1,0:T(8,128)(2,1)S(1)} %select_n.41), channel_id=1, source_target_pairs={{0,1},{1,0},{2,3},{3,2},{4,5},{5,4},{6,7},{7,6},{16,17},{17,16},{1... | collective-permute-start | bytes 221192 | tf_op jit(solution)/shard_map/ppermute | solution.py:242
  5.4 0.1 copy.8
  5.5 0.8 %collective-permute-done.1.refs_1_ = bf16[96,384]{1,0:T(8,128)(2,1)S(1)} collective-permute-done((bf16[96,384]{1,0:T(8,128)(2,1)S(1)}, bf16[96,384]{1,0:T(8,128)(2,1)S(1)}, u32[]{:S(2)}, u32[]{:S(2)}) %collective-permute-start.1) | collective-permute-done | bytes 73760 | tf_op jit(solution)/shard_map/ppermute | solution.py:242
  6.3 4.0 %collective-permute-start.2 = (bf16[2,96,384]{2,1,0:T(8,128)(2,1)S(1)}, bf16[2,96,384]{2,1,0:T(8,128)(2,1)S(1)}, u32[]{:S(2)}, u32[]{:S(2)}) collective-permute-start(bf16[2,96,384]{2,1,0:T(8,128)(2,1)S(1)} %pad_maximum_fusion), channel_id=1, source_target_pairs={{0,2},{1,3},{2,0},{3,1},{4,6},{5,7},{6,4},{7,5},{16,18},{17,19},{1... | collective-permute-start | bytes 442376 | tf_op jit(solution)/shard_map/ppermute | solution.py:242
  10.3 0.0 copy-done.3
  10.3 5.8 %collective-permute-start = (s32[16,512]{1,0:T(8,128)S(1)}, s32[16,512]{1,0:T(8,128)S(1)}, u32[]{:S(2)}, u32[]{:S(2)}) collective-permute-start(s32[16,512]{1,0:T(8,128)S(1)} %copy-done.3), channel_id=1, source_target_pairs={{0,4},{1,5},{6,2},{7,3},{4,8},{5,9},{10,6},{11,7},{8,12},{9,13},{1... | collective-permute-start | bytes 98312 | tf_op jit(solution)/shard_map/ppermute | solution.py:221
  16.2 0.0 copy-start.1
  16.2 0.0 copy-start.2
  16.2 0.0 collective-permute-done.2.refs_2_
  16.2 0.7 %collective-permute-start.5 = (bf16[96,384]{1,0:T(8,128)(2,1)S(1)}, bf16[96,384]{1,0:T(8,128)(2,1)S(1)}, u32[]{:S(2)}, u32[]{:S(2)}) collective-permute-start(bf16[96,384]{1,0:T(8,128)(2,1)S(1)} %select_n.41), channel_id=1, source_target_pairs={{8,11},{9,10},{10,9},{11,8},{12,15},{13,14},{14,13},{15,12},{24,27... | collective-permute-start | bytes 221192 | tf_op jit(solution)/shard_map/ppermute | solution.py:242
  16.9 0.7 %collective-permute-start.3 = (bf16[96,384]{1,0:T(8,128)(2,1)S(1)}, bf16[96,384]{1,0:T(8,128)(2,1)S(1)}, u32[]{:S(2)}, u32[]{:S(2)}) collective-permute-start(bf16[96,384]{1,0:T(8,128)(2,1)S(1)} %select_n.41), channel_id=1, source_target_pairs={{8,9},{9,8},{10,11},{11,10},{12,13},{13,12},{14,15},{15,14},{24,25... | collective-permute-start | bytes 221192 | tf_op jit(solution)/shard_map/ppermute | solution.py:242
  17.5 0.7 %collective-permute-start.4 = (bf16[96,384]{1,0:T(8,128)(2,1)S(1)}, bf16[96,384]{1,0:T(8,128)(2,1)S(1)}, u32[]{:S(2)}, u32[]{:S(2)}) collective-permute-start(bf16[96,384]{1,0:T(8,128)(2,1)S(1)} %select_n.39.refs_0_), channel_id=1, source_target_pairs={{8,10},{9,11},{10,8},{11,9},{12,14},{13,15},{14,12},{15,13},{24,26... | collective-permute-start | bytes 221192 | tf_op jit(solution)/shard_map/ppermute | solution.py:242
  18.2 3.1 %collective-permute-done.near_ref = s32[16,512]{1,0:T(8,128)S(1)} collective-permute-done((s32[16,512]{1,0:T(8,128)S(1)}, s32[16,512]{1,0:T(8,128)S(1)}, u32[]{:S(2)}, u32[]{:S(2)}) %collective-permute-start) | collective-permute-done | bytes 32800 | tf_op jit(solution)/shard_map/ppermute | solution.py:221
  21.3 0.3 band.1.b_ref
  21.6 0.0 collective-permute-done.4.refs_4_
  21.6 0.0 collective-permute-done.5.refs_5_
  21.7 0.0 collective-permute-done.3.refs_3_
  21.7 0.0 copy-done.1
  21.7 0.0 copy-done.2
  21.7 4.4 %image.1 = bf16[80,512]{1,0:T(8,128)(2,1)S(1)} custom-call(f32[4,560,128]{2,1,0:T(8,128)S(1)} %band.1.b_ref, bf16[96,384]{1,0:T(8,128)(2,1)S(1)} %select_n.39.refs_0_, bf16[96,384]{1,0:T(8,128)(2,1)S(1)} %collective-permute-done.1.refs_1_, bf16[2,96,384]{2,1,0:T(8,128)(2,1)S(1)} %collective-permute-done.2.refs_2_, ...), custom_call_target="tpu_custom_call" | custom-call | tf_op jit(solution)/shard_map/image/pallas_call | solution.py:260
  26.1 7.6 %all-gather = bf16[320,512]{1,0:T(8,128)(2,1)S(1)} all-gather(bf16[80,512]{1,0:T(8,128)(2,1)S(1)} %image.1), channel_id=2, replica_groups=mesh['tile'=128,'src'=4] {'src'}, dimensions={0}, use_global_device_ids=true | all-gather | bytes 409600 | tf_op jit(solution)/shard_map/all_gather | solution.py:269
  33.7 4.7 %bake.1 = (f32[2,16,512]{2,1,0:T(8,128)}, f32[2,16,512]{2,1,0:T(8,128)}) custom-call(bf16[4,80,512]{2,1,0:T(8,128)(2,1)S(1)} %bitcast.16), custom_call_target="tpu_custom_call" | custom-call | tf_op jit(solution)/shard_map/bake/pallas_call | solution.py:276
  (6 shorter events, 0.1 us)
Async XLA Ops:
  0.6 1.2 %copy-start = (bf16[4,3,8,2,17,17]{5,3,4,2,1,0:T(2,128)(2,1)S(1)}, bf16[4,3,8,2,17,17]{5,3,4,2,1,0:T(2,128)(2,1)}, u32[]{:S(2)}) copy-start(bf16[4,3,8,2,17,17]{5,3,4,2,1,0:T(2,128)(2,1)} %param.6) | copy-start | bytes 332932
  2.6 7.7 %copy-start.3 = (s32[16,512]{1,0:T(8,128)S(1)}, s32[16,512]{1,0:T(8,128)}, u32[]{:S(2)}) copy-start(s32[16,512]{1,0:T(8,128)} %mask_ref.1) | copy-start | bytes 98308
  2.8 3.5 %collective-permute-start.1 = (bf16[96,384]{1,0:T(8,128)(2,1)S(1)}, bf16[96,384]{1,0:T(8,128)(2,1)S(1)}, u32[]{:S(2)}, u32[]{:S(2)}) collective-permute-start(bf16[96,384]{1,0:T(8,128)(2,1)S(1)} %select_n.41), channel_id=1, source_target_pairs={{0,1},{1,0},{2,3},{3,2},{4,5},{5,4},{6,7},{7,6},{16,17},{17,16},{1... | collective-permute-start | bytes 221192 | tf_op jit(solution)/shard_map/ppermute | solution.py:242
  6.3 9.9 %collective-permute-start.2 = (bf16[2,96,384]{2,1,0:T(8,128)(2,1)S(1)}, bf16[2,96,384]{2,1,0:T(8,128)(2,1)S(1)}, u32[]{:S(2)}, u32[]{:S(2)}) collective-permute-start(bf16[2,96,384]{2,1,0:T(8,128)(2,1)S(1)} %pad_maximum_fusion), channel_id=1, source_target_pairs={{0,2},{1,3},{2,0},{3,1},{4,6},{5,7},{6,4},{7,5},{16,18},{17,19},{1... | collective-permute-start | bytes 442376 | tf_op jit(solution)/shard_map/ppermute | solution.py:242
  10.3 11.0 %collective-permute-start = (s32[16,512]{1,0:T(8,128)S(1)}, s32[16,512]{1,0:T(8,128)S(1)}, u32[]{:S(2)}, u32[]{:S(2)}) collective-permute-start(s32[16,512]{1,0:T(8,128)S(1)} %copy-done.3), channel_id=1, source_target_pairs={{0,4},{1,5},{6,2},{7,3},{4,8},{5,9},{10,6},{11,7},{8,12},{9,13},{1... | collective-permute-start | bytes 98312 | tf_op jit(solution)/shard_map/ppermute | solution.py:221
  16.2 5.5 %copy-start.1 = (f32[2]{0:T(128)S(1)}, f32[2]{0:T(128)}, u32[]{:S(2)}) copy-start(f32[2]{0:T(128)} %refs_6_.1) | copy-start | bytes 28
  16.2 5.5 %copy-start.2 = (f32[2]{0:T(128)S(1)}, f32[2]{0:T(128)}, u32[]{:S(2)}) copy-start(f32[2]{0:T(128)} %refs_7_.1) | copy-start | bytes 28
  16.2 5.5 %collective-permute-start.5 = (bf16[96,384]{1,0:T(8,128)(2,1)S(1)}, bf16[96,384]{1,0:T(8,128)(2,1)S(1)}, u32[]{:S(2)}, u32[]{:S(2)}) collective-permute-start(bf16[96,384]{1,0:T(8,128)(2,1)S(1)} %select_n.41), channel_id=1, source_target_pairs={{8,11},{9,10},{10,9},{11,8},{12,15},{13,14},{14,13},{15,12},{24,27... | collective-permute-start | bytes 221192 | tf_op jit(solution)/shard_map/ppermute | solution.py:242
  16.9 4.8 %collective-permute-start.3 = (bf16[96,384]{1,0:T(8,128)(2,1)S(1)}, bf16[96,384]{1,0:T(8,128)(2,1)S(1)}, u32[]{:S(2)}, u32[]{:S(2)}) collective-permute-start(bf16[96,384]{1,0:T(8,128)(2,1)S(1)} %select_n.41), channel_id=1, source_target_pairs={{8,9},{9,8},{10,11},{11,10},{12,13},{13,12},{14,15},{15,14},{24,25... | collective-permute-start | bytes 221192 | tf_op jit(solution)/shard_map/ppermute | solution.py:242
  17.5 4.1 %collective-permute-start.4 = (bf16[96,384]{1,0:T(8,128)(2,1)S(1)}, bf16[96,384]{1,0:T(8,128)(2,1)S(1)}, u32[]{:S(2)}, u32[]{:S(2)}) collective-permute-start(bf16[96,384]{1,0:T(8,128)(2,1)S(1)} %select_n.39.refs_0_), channel_id=1, source_target_pairs={{8,10},{9,11},{10,8},{11,9},{12,14},{13,15},{14,12},{15,13},{24,26... | collective-permute-start | bytes 221192 | tf_op jit(solution)/shard_map/ppermute | solution.py:242
